TPU v7x, 768 devices: a whole 4x8x12 slice. The times are simulated.
768 devices in a mesh: px: 96 (over z, y_hi, x), py: 8 (over y_lo, core).
Axes of the slice: x: 4, y: 8 (y_hi: 2, y_lo: 4; y = y_hi * 4 + y_lo), z: 12, core: 2. Of those that a mesh axis runs over, the one named last changes fastest.
Arguments:
- displacement: float32 [3, 384, 128, 128], P(None, 'px', 'py'), may hold values from -6 to 6
- velocity: float32 [3, 384, 128, 128], P(None, 'px', 'py'), may hold values from -6 to 6
- inverse_mass: float32 [384, 128, 128], P('px', 'py'), may hold values from 0.5 to 2
- lame_first: float32 [5, 5, 5, 96, 1024], P(None, None, None, 'px', 'py'), may hold values from 0.5 to 2
- lame_second: float32 [5, 5, 5, 96, 1024], P(None, None, None, 'px', 'py'), may hold values from 0.5 to 2
- level_map: int32 [96, 1024], P('px', 'py'), may hold values from 0 to 2, as said below
Outputs:
- new_displacement: float32 [3, 384, 128, 128], P(None, 'px', 'py')
- new_velocity: float32 [3, 384, 128, 128], P(None, 'px', 'py')
Inputs may be any that keep to these rules, and one draw needn't show every extreme that they name: `level_map`: level 2 is the finest. The device whose blocks hold the most finest-level elements holds exactly 96 of them; no device holds more.
All inputs are finite; a program needn't handle non-finite values.
Results may differ from a plain program's by a relative error of at most 0.0003.
Values sent between devices are 32-bit elements; how exact they have to be, the bound alone decides.
A program may use at most 32 MiB of HBM per device.

v0:
```python
import functools

import jax
import jax.numpy as jnp
import ml_dtypes
import numpy as np
from jax import lax
from jax.experimental import pallas as pl
from jax.experimental.pallas import tpu as pltpu
from jax.sharding import PartitionSpec as P

SUBSTEPS = 4
TIME_STEP = 0.1
MESH = pl.DeviceIdType.MESH
F32 = jnp.float32
BF16 = jnp.bfloat16
NEIGHBOURS = [(1, 0), (-1, 0), (1, 1), (1, -1), (-1, 1), (-1, -1), (0, 1), (0, -1)]
SLOT = {d: n for n, d in enumerate(NEIGHBOURS)}
XF, XB, DPP, DPM, DMP, DMM, YU, YD = range(8)


def gll_tables():
    points = np.array([-1.0, -np.sqrt(3.0 / 7.0), 0.0, np.sqrt(3.0 / 7.0), 1.0])
    weights = np.array([0.1, 49.0 / 90.0, 32.0 / 45.0, 49.0 / 90.0, 0.1])
    legendre = (35.0 * points**4 - 30.0 * points**2 + 3.0) / 8.0
    derivative = np.zeros((5, 5))
    for row in range(5):
        for col in range(5):
            if row != col:
                derivative[row, col] = legendre[row] / (legendre[col] * (points[row] - points[col]))
    derivative[0, 0] = -5.0
    derivative[4, 4] = 5.0
    return derivative, weights


def place(k, j):
    if k < 4 and j < 4:
        return k * 4 + j
    return 16 + k if k < 4 else 20 + j


def split_table(table):
    high = table.astype(ml_dtypes.bfloat16)
    low = (table - high.astype(np.float64)).astype(ml_dtypes.bfloat16)
    return high, low


@functools.cache
def tables():
    derivative, weights = gll_tables()
    grads = np.zeros((384, 208))
    cube = np.zeros(384)
    for i in range(5):
        for j in range(5):
            for k in range(5):
                row = i * 25 + j * 5 + k
                for d in range(3):
                    cube[d * 128 + row] = weights[i] * weights[j] * weights[k]
                for n in range(5):
                    grads[row, place(k, j) * 8 + n] += derivative[i, n]
                    grads[128 + row, place(k, n) * 8 + i] += derivative[j, n]
                    grads[256 + row, place(n, j) * 8 + i] += derivative[k, n]
    high, low = split_table(grads)
    first = np.concatenate([high, high, low], axis=1)
    high, low = split_table((grads[:, :200] * cube[:, None]).T)
    second = np.concatenate([high, high, low], axis=1)
    spread = np.zeros((512, 512), ml_dtypes.bfloat16)
    pack = np.zeros((128, 128), ml_dtypes.bfloat16)
    for k in range(4):
        for c in range(32):
            pack[4 * c + k, k * 32 + c] = 1
            for b in range(4):
                spread[b * 128 + 4 * c + k, k * 128 + b * 32 + c] = 1
    return first, second, spread, np.ascontiguousarray(spread.T), pack


def halves(value):
    high = value.astype(BF16)
    return high, (value - high.astype(F32)).astype(BF16)


def permute(value, matrix):
    high, low = halves(value)
    rows = value.shape[0]
    out = jnp.dot(jnp.concatenate([high, low], axis=0), matrix, preferred_element_type=F32)
    return out[:rows] + out[rows:]


def kernel(
    nx,
    ny,
    u_hbm,
    v_hbm,
    im_hbm,
    la_hbm,
    mu_hbm,
    level_hbm,
    first_hbm,
    second_hbm,
    spread_hbm,
    gather_hbm,
    pack_hbm,
    uo_hbm,
    vo_hbm,
    u_vm,
    vim_vm,
    la_vm,
    mu_vm,
    level_vm,
    first_vm,
    second_vm,
    spread_vm,
    gather_vm,
    pack_vm,
    halo_u,
    halo_vim,
    halo_y_send,
    halo_y,
    halo_c_send,
    halo_c,
    x_own,
    x_line,
    u_all,
    v_own,
    im_own,
    u_line,
    v_line,
    im_line,
    u_split,
    s_split,
    f_kept,
    f_sum,
    pack_up,
    pack_down,
    send_x,
    send_d,
    send_y,
    recv_x,
    recv_d,
    recv_y,
    uo_vm,
    vo_vm,
    load_sem,
    halo_send_sem,
    halo_recv_sem,
    send_sem,
    recv_sem,
):
    px, py = lax.axis_index("px"), lax.axis_index("py")

    def present(dx, dy):
        conditions = []
        if dx:
            conditions.append(px < nx - 1 if dx > 0 else px > 0)
        if dy:
            conditions.append(py < ny - 1 if dy > 0 else py > 0)
        return functools.reduce(jnp.logical_and, conditions)

    barrier = pltpu.get_barrier_semaphore()
    for dx, dy in NEIGHBOURS:

        @pl.when(present(dx, dy))
        def _():
            pl.semaphore_signal(barrier, inc=1, device_id=(px + dx, py + dy), device_id_type=MESH)

    loads = []
    for n, (source, target) in enumerate(
        [
            (u_hbm, u_vm),
            (v_hbm, vim_vm.at[0:3]),
            (im_hbm, vim_vm.at[3:4]),
            (spread_hbm, spread_vm),
            (pack_hbm, pack_vm),
            (first_hbm, first_vm),
            (la_hbm, la_vm.at[0:125]),
            (mu_hbm, mu_vm.at[0:125]),
            (second_hbm, second_vm),
            (level_hbm, level_vm),
            (gather_hbm, gather_vm),
        ]
    ):
        loads.append(pltpu.make_async_copy(source, target, load_sem.at[n]))
        loads[-1].start()

    x_own[...] = jnp.zeros_like(x_own)
    x_line[...] = jnp.zeros_like(x_line)
    u_all[...] = jnp.zeros_like(u_all)

    for n, (dx, dy) in enumerate(NEIGHBOURS):

        @pl.when(jnp.logical_not(present(-dx, -dy)))
        def _():
            for s in range(SUBSTEPS):
                if n < 2:
                    recv_x[s, n] = jnp.zeros_like(recv_x[s, n])
                elif n < 6:
                    recv_d[s, n - 2] = jnp.zeros_like(recv_d[s, n - 2])
                else:
                    recv_y[s, n - 6] = jnp.zeros_like(recv_y[s, n - 6])
            if n == XB:
                halo_u[...] = jnp.zeros_like(halo_u)
                halo_vim[...] = jnp.zeros_like(halo_vim)
            if n == YD:
                halo_y[...] = jnp.zeros_like(halo_y)
            if n == DMM:
                halo_c[...] = jnp.zeros_like(halo_c)

    for n in range(3):
        loads[n].wait()
    for c in range(7):
        source = u_vm.at[c] if c < 3 else vim_vm.at[c - 3]
        halo_y_send[4 * c : 4 * c + 4, :] = source[pl.ds(0, 4, stride=16), :]
        halo_c_send[c : c + 1, :] = source[0:1, :]

    def remote(source, target, sems, n, dx, dy):
        send, recv = sems
        return pltpu.make_async_remote_copy(
            src_ref=source,
            dst_ref=target,
            send_sem=send.at[n],
            recv_sem=recv.at[n],
            device_id=(px + dx, py + dy),
            device_id_type=MESH,
        )

    halo_sems = (halo_send_sem, halo_recv_sem)
    halos = [
        remote(u_hbm.at[:, 0:16, :], halo_u, halo_sems, 0, -1, 0),
        remote(halo_c_send, halo_c, halo_sems, 1, -1, -1),
        remote(halo_y_send, halo_y, halo_sems, 2, 0, -1),
        remote(v_hbm.at[:, 0:16, :], halo_vim.at[0:3], halo_sems, 3, -1, 0),
        remote(im_hbm.at[:, 0:16, :], halo_vim.at[3:4], halo_sems, 4, -1, 0),
    ]
    halo_to = [(-1, 0), (-1, -1), (0, -1), (-1, 0), (-1, 0)]

    neighbours = 0
    for dx, dy in NEIGHBOURS:
        neighbours = neighbours + present(dx, dy).astype(jnp.int32)
    pl.semaphore_wait(barrier, neighbours)
    for copy, to in zip(halos, halo_to):

        @pl.when(present(*to))
        def _():
            copy.start()

    def wait_halo(n):
        dx, dy = halo_to[n]

        @pl.when(present(-dx, -dy))
        def _():
            halos[n].wait_recv()

    lane = lax.broadcasted_iota(jnp.int32, (8, 128), 1)
    sublane = lax.broadcasted_iota(jnp.int32, (8, 128), 0)
    depth = lane & 31
    column = lane >> 5

    def fill_own(c, source):
        for j in range(4):
            for b in range(4):
                row = (c * 4 + j) * 8
                x_own[b, row : row + 4, :] = source[pl.ds(4 * b + j, 4, stride=16), :]

    def fill_far(c, source):
        for b in range(4):
            x_own[b, pl.ds(c * 32 + 4, 4, stride=8), :] = source[4 * b : 4 * b + 4, :]

    def spread(first_row, rows):
        wide = jnp.concatenate([x_own[b, first_row : first_row + rows, :] for b in range(4)], axis=1)
        return permute(wide, spread_vm[...])

    for c in range(3):
        fill_own(c, u_vm.at[c])
    for c in range(4):
        fill_own(3 + c, vim_vm.at[c])
    loads[3].wait()
    loads[4].wait()
    for n in range(5, 11):
        loads[n].wait()
    la_vm[125:128, :] = jnp.zeros((3, 128), F32)
    mu_vm[125:128, :] = jnp.zeros((3, 128), F32)

    wait_halo(0)
    wait_halo(1)
    wait_halo(2)
    for c in range(3):
        fill_far(c, halo_u.at[c])
    for c in range(7):
        x_line[c * 8 : c * 8 + 4, :] = halo_y[4 * c : 4 * c + 4, :]
        x_line[c * 8 + 4 : c * 8 + 5, :] = halo_c[c : c + 1, :]
    nodes = spread(0, 96)
    for c in range(3):
        for j in range(4):
            for k in range(4):
                row = (c * 4 + j) * 8
                u_all[c, (k * 4 + j) * 8 : (k * 4 + j + 1) * 8, :] = nodes[row : row + 8, k * 128 : (k + 1) * 128]
    lines = permute(x_line[...], pack_vm[...])
    u_line[...] = lines[0:24]
    v_line[...] = lines[24:48]
    im_line[...] = TIME_STEP * lines[48:56]

    def group(p):
        return pl.ds(p * 8, 8)

    def expand():
        for c in range(3):
            line = u_line[c * 8 : c * 8 + 8, :]
            for k in range(4):
                inner = pltpu.roll(u_all[c, group(k * 4), :], 96, 1)
                outer = pltpu.roll(line, (96 - 32 * k) % 128, 1) if k != 3 else line
                u_all[c, group(16 + k), :] = jnp.where(column == 3, outer, inner)
            for j in range(5):
                below = pltpu.roll(u_all[c, group(j if j < 4 else 16), :], 127, 1)
                u_all[c, group(20 + j), :] = jnp.where(depth < 31, below, 0.0)

    def forces(s):
        for c in range(3):
            high, low = halves(u_all[c])
            lanes = slice(c * 128, (c + 1) * 128)
            u_split[0:208, lanes] = high
            u_split[208:416, lanes] = low
            u_split[416:624, lanes] = high
        grads = jnp.dot(first_vm[...], u_split[...], preferred_element_type=F32)

        def grad(c, d):
            return grads[d * 128 : (d + 1) * 128, c * 128 : (c + 1) * 128]

        first, second = la_vm[...], mu_vm[...]
        pressure = first * (grad(0, 0) + grad(1, 1) + grad(2, 2))
        for c in range(3):
            for d in range(c, 3):
                if c == d:
                    stress = pressure + 2.0 * second * grad(c, c)
                else:
                    stress = second * (grad(c, d) + grad(d, c))
                high, low = halves(stress)
                for e, f in ((c, d), (d, c))[: 1 + (c != d)]:
                    lanes = slice(e * 128, (e + 1) * 128)
                    s_split[f * 128 : (f + 1) * 128, lanes] = high
                    s_split[384 + f * 128 : 384 + (f + 1) * 128, lanes] = low
                    s_split[768 + f * 128 : 768 + (f + 1) * 128, lanes] = high
        out = jnp.dot(second_vm[...], s_split[...], preferred_element_type=F32)
        least = jnp.where(s == 0, 0, jnp.where(s == 2, 1, 2))
        active = level_vm[...] >= least
        for c in range(3):
            new = out[:, c * 128 : (c + 1) * 128]
            f_kept[c] = jnp.where(active, new, f_kept[c])

    def assemble(s, last):
        for c in range(3):
            f = [f_kept[c, group(p), :] for p in range(25)]
            for j in range(5):
                p = j if j < 4 else 16
                f[p] = f[p] + jnp.where(depth > 0, pltpu.roll(f[20 + j], 1, 1), 0.0)
            up = jnp.zeros((8, 128), F32)
            down = jnp.zeros((8, 128), F32)
            for k in range(4):
                shifted = pltpu.roll(f[16 + k], 32, 1)
                up = jnp.where(column == k, pltpu.roll(shifted, 32 * k, 1) if k else shifted, up)
                down = jnp.where(column == k, pltpu.roll(f[4 * k], 32 * k, 1) if k else f[0], down)
                f[4 * k] = f[4 * k] + jnp.where(column > 0, shifted, 0.0)
            for p in range(16):
                f_sum[c, group(p), :] = f[p]
            pack_up[c * 8 : c * 8 + 8, :] = up
            pack_down[c * 8 : c * 8 + 8, :] = down
        for c in range(3):
            send_x[s, XF, c * 16 : c * 16 + 16, :] = f_sum[c, pl.ds(4, 16, stride=8), :]
            if not last:
                send_x[s, XB, c * 16 : c * 16 + 16, :] = f_sum[c, pl.ds(0, 16, stride=8), :]
        up_far = pack_up[pl.ds(4, 3, stride=8), :]
        send_d[s, DPP - 2, 0:3, :] = up_far
        send_y[s, 0] = pack_up[...]
        if not last:
            up_near = pack_up[pl.ds(0, 3, stride=8), :]
            send_d[s, DPM - 2, 0:3, :] = pack_down[pl.ds(4, 3, stride=8), :]
            send_d[s, DMP - 2, 0:3, :] = up_near
            send_d[s, DMM - 2, 0:3, :] = pack_down[pl.ds(0, 3, stride=8), :]
            send_x[s, XF, 48:51, :] = up_far
            send_x[s, XB, 48:51, :] = up_near
            send_y[s, 1] = pack_down[...]

    def exchange(s, last):
        copies = []
        for n, (dx, dy) in enumerate(NEIGHBOURS):
            if last and (dx < 0 or dy < 0):
                continue
            if n < 2:
                pair = (send_x.at[s, n], recv_x.at[s, n])
            elif n < 6:
                pair = (send_d.at[s, n - 2], recv_d.at[s, n - 2])
            else:
                pair = (send_y.at[s, n - 6], recv_y.at[s, n - 6])
            copies.append(((dx, dy), remote(*pair, (send_sem.at[s], recv_sem.at[s]), n, dx, dy)))
        return copies

    def start(copies):
        for to, copy in copies:

            @pl.when(present(*to))
            def _():
                copy.start()

    def arrive(copies):
        for (dx, dy), copy in copies:

            @pl.when(present(-dx, -dy))
            def _():
                copy.wait_recv()

    def finish(copies):
        for to, copy in copies:

            @pl.when(present(*to))
            def _():
                copy.wait_send()

    def advance(s, last):
        for c in range(3):
            near = recv_y[s, 0, c * 8 : c * 8 + 8, :]
            near = near + jnp.where(sublane == 0, recv_d[s, DPP - 2, c : c + 1, :], 0.0)
            if not last:
                near = near + jnp.where(sublane == 4, recv_d[s, DMP - 2, c : c + 1, :], 0.0)
            for k in range(4):
                part = pltpu.roll(near, 128 - 32 * k, 1) if k else near
                f_sum[c, group(4 * k), :] = f_sum[c, group(4 * k), :] + jnp.where(column == 0, part, 0.0)
            f_sum[c, pl.ds(0, 16, stride=8), :] = f_sum[c, pl.ds(0, 16, stride=8), :] + recv_x[s, XF, c * 16 : c * 16 + 16, :]
            if not last:
                f_sum[c, pl.ds(4, 16, stride=8), :] = (
                    f_sum[c, pl.ds(4, 16, stride=8), :] + recv_x[s, XB, c * 16 : c * 16 + 16, :]
                )
        for c in range(3):
            v = v_own[c] - im_own[...] * f_sum[c]
            v_own[c] = v
            u_all[c, 0:128, :] = u_all[c, 0:128, :] + TIME_STEP * v
        if last:
            return
        for c in range(3):
            rows = slice(c * 8, c * 8 + 8)
            far = pack_up[rows, :] + recv_y[s, 1, rows, :]
            left = recv_x[s, XF, 48 + c : 49 + c, :] + recv_d[s, DPM - 2, c : c + 1, :]
            right = recv_x[s, XB, 48 + c : 49 + c, :] + recv_d[s, DMM - 2, c : c + 1, :]
            far = far + jnp.where(sublane == 0, left, 0.0) + jnp.where(sublane == 4, right, 0.0)
            v = v_line[rows, :] - im_line[...] * far
            v_line[rows, :] = v
            u_line[rows, :] = u_line[rows, :] + TIME_STEP * v
        expand()

    def late_nodes():
        wait_halo(3)
        wait_halo(4)
        for c in range(4):
            fill_far(3 + c, halo_vim.at[c])
        values = spread(96, 128)
        for c in range(4):
            for j in range(4):
                for k in range(4):
                    row = (c * 4 + j) * 8
                    value = values[row : row + 8, k * 128 : (k + 1) * 128]
                    if c < 3:
                        v_own[c, group(k * 4 + j), :] = value
                    else:
                        im_own[group(k * 4 + j), :] = TIME_STEP * value

    expand()
    forces(0)
    assemble(0, False)
    copies = exchange(0, False)
    start(copies)
    late_nodes()
    arrive(copies)
    advance(0, False)

    def substep(s, carry):
        forces(s)
        assemble(s, False)
        copies = exchange(s, False)
        start(copies)
        arrive(copies)
        advance(s, False)
        return carry

    lax.fori_loop(1, SUBSTEPS - 1, substep, 0)
    s = SUBSTEPS - 1
    forces(s)
    assemble(s, True)
    copies = exchange(s, True)
    start(copies)
    arrive(copies)
    advance(s, True)

    rows = []
    for source in (u_all, v_own):
        for c in range(3):
            for j in range(4):
                rows.append(jnp.concatenate([source[c, group(k * 4 + j), :] for k in range(4)], axis=1))
    result = permute(jnp.concatenate(rows, axis=0), gather_vm[...])
    for a, target in enumerate((uo_vm, vo_vm)):
        for c in range(3):
            for j in range(4):
                row = ((a * 3 + c) * 4 + j) * 8
                for b in range(4):
                    target[c, pl.ds(4 * b + j, 4, stride=16), :] = result[row : row + 4, b * 128 : (b + 1) * 128]
    stores = [
        pltpu.make_async_copy(uo_vm, uo_hbm, load_sem.at[0]),
        pltpu.make_async_copy(vo_vm, vo_hbm, load_sem.at[1]),
    ]
    for copy in stores:
        copy.start()
    for copy, to in zip(halos, halo_to):

        @pl.when(present(*to))
        def _():
            copy.wait_send()

    def drain(s, carry):
        finish(exchange(s, False))
        return carry

    lax.fori_loop(0, SUBSTEPS - 1, drain, 0)
    finish(exchange(SUBSTEPS - 1, True))
    for copy in stores:
        copy.wait()


def shards(nx, ny, displacement, velocity, inverse_mass, lame_first, lame_second, level_map):
    first, second, spread, gather, pack = (jnp.asarray(table) for table in tables())
    vmem = pltpu.VMEM
    uo, vo = pl.pallas_call(
        functools.partial(kernel, nx, ny),
        out_shape=[jax.ShapeDtypeStruct((3, 64, 128), F32)] * 2,
        in_specs=[pl.BlockSpec(memory_space=pl.ANY)] * 11,
        out_specs=[pl.BlockSpec(memory_space=pl.ANY)] * 2,
        scratch_shapes=[
            vmem((3, 64, 128), F32),
            vmem((4, 64, 128), F32),
            vmem((128, 128), F32),
            vmem((128, 128), F32),
            vmem((1, 128), jnp.int32),
            vmem((384, 624), BF16),
            vmem((200, 1152), BF16),
            vmem((512, 512), BF16),
            vmem((512, 512), BF16),
            vmem((128, 128), BF16),
            vmem((3, 16, 128), F32),
            vmem((4, 16, 128), F32),
            vmem((32, 128), F32),
            vmem((32, 128), F32),
            vmem((8, 128), F32),
            vmem((8, 128), F32),
            vmem((4, 224, 128), F32),
            vmem((56, 128), F32),
            vmem((3, 208, 128), F32),
            vmem((3, 128, 128), F32),
            vmem((128, 128), F32),
            vmem((24, 128), F32),
            vmem((24, 128), F32),
            vmem((8, 128), F32),
            vmem((624, 384), BF16),
            vmem((1152, 384), BF16),
            vmem((3, 200, 128), F32),
            vmem((3, 128, 128), F32),
            vmem((24, 128), F32),
            vmem((24, 128), F32),
            vmem((SUBSTEPS, 2, 56, 128), F32),
            vmem((SUBSTEPS, 4, 8, 128), F32),
            vmem((SUBSTEPS, 2, 24, 128), F32),
            vmem((SUBSTEPS, 2, 56, 128), F32),
            vmem((SUBSTEPS, 4, 8, 128), F32),
            vmem((SUBSTEPS, 2, 24, 128), F32),
            vmem((3, 64, 128), F32),
            vmem((3, 64, 128), F32),
            pltpu.SemaphoreType.DMA((11,)),
            pltpu.SemaphoreType.DMA((5,)),
            pltpu.SemaphoreType.DMA((5,)),
            pltpu.SemaphoreType.DMA((SUBSTEPS, 8)),
            pltpu.SemaphoreType.DMA((SUBSTEPS, 8)),
        ],
        compiler_params=pltpu.CompilerParams(collective_id=0, has_side_effects=True),
        name="substeps",
    )(
        displacement.reshape(3, 64, 128),
        velocity.reshape(3, 64, 128),
        inverse_mass.reshape(1, 64, 128),
        lame_first.reshape(125, 128),
        lame_second.reshape(125, 128),
        level_map,
        first,
        second,
        spread,
        gather,
        pack,
    )
    return uo.reshape(3, 4, 16, 128), vo.reshape(3, 4, 16, 128)


def solution(mesh):
    in_specs = (
        P(None, "px", "py", None),
        P(None, "px", "py", None),
        P("px", "py", None),
        P(None, None, None, "px", "py"),
        P(None, None, None, "px", "py"),
        P("px", "py"),
    )
    out_specs = (P(None, "px", "py", None), P(None, "px", "py", None))
    body = functools.partial(shards, mesh.shape["px"], mesh.shape["py"])
    return jax.shard_map(body, mesh=mesh, in_specs=in_specs, out_specs=out_specs, check_vma=False)
```

profile of v0, /device:TPU:513, one launch (start us, length us, event | category | flops | bytes accessed | tf_op | source)
XLA Modules:
  0.0 55.9 jit_solution(178322811361481651)
XLA Ops:
  0.6 1.0 %reduce = f32[5,5,5,128]{3,2,1,0:T(8,128)S(1)} reduce(f32[5,5,5,1,128]{4,3,2,1,0:T(1,128)} %param.14, f32[]{:T(128)} %constant.21), dimensions={3}, to_apply=%param.14.reduce_sub_computation | reduce | bytes 128004 | tf_op args[3]
  1.6 0.0 copy-start.1
  1.6 0.6 %reshape.28.la_hbm = f32[125,128]{1,0:T(8,128)} reshape(f32[5,5,5,128]{3,2,1,0:T(8,128)S(1)} %reduce) | data formatting | bytes 128000 | tf_op jit(solution)/shard_map/reshape | solution.py:584
  2.3 0.2 copy-done.1
  2.5 0.2 reduce.1
  2.6 0.6 %reshape.29.mu_hbm = f32[125,128]{1,0:T(8,128)} reshape(f32[5,5,5,128]{3,2,1,0:T(8,128)S(1)} %reduce.1) | data formatting | bytes 128000 | tf_op jit(solution)/shard_map/reshape | solution.py:585
  3.3 50.4 %substeps.1 = (f32[3,64,128]{2,1,0:T(8,128)}, f32[3,64,128]{2,1,0:T(8,128)}) custom-call(f32[3,64,128]{2,1,0:T(8,128)} %bitcast.5, f32[3,64,128]{2,1,0:T(8,128)} %bitcast.6, f32[1,64,128]{2,1,0:T(8,128)} %bitcast.9, f32[125,128]{1,0:T(8,128)} %reshape.28.la_hbm, f32[125,128]{1,0:T(8,128)} %reshape.29.mu_hbm, s32[1,128]{1,0:T(1,128)} %level_hbm.1, ...), custom_call_target="tpu_custom_call" | custom-call | tf_op jit(solution)/shard_map/substeps/pallas_call | solution.py:528
  53.7 0.0 copy-start
  53.7 1.6 %copy.17 = f32[3,4,16,128]{3,2,1,0:T(8,128)} copy(f32[3,4,16,128]{3,2,1,0:T(8,128)} %bitcast.8) | data formatting | bytes 196608
  55.3 0.0 copy-done
  55.3 0.6 %copy.18 = f32[3,4,16,128]{3,2,1,0:T(8,128)} copy(f32[3,4,16,128]{3,2,1,0:T(8,128)S(1)} %bitcast.7) | data formatting | bytes 196608
Async XLA Ops:
  1.6 0.8 %copy-start.1 = (f32[5,5,5,1,128]{4,3,2,1,0:T(1,128)S(1)}, f32[5,5,5,1,128]{4,3,2,1,0:T(1,128)}, u32[]{:S(2)}) copy-start(f32[5,5,5,1,128]{4,3,2,1,0:T(1,128)} %param.15) | copy-start | bytes 192004
  53.7 1.6 %copy-start = (f32[3,64,128]{2,1,0:T(8,128)S(1)}, f32[3,64,128]{2,1,0:T(8,128)}, u32[]{:S(2)}) copy-start(f32[3,64,128]{2,1,0:T(8,128)} %get-tuple-element.5) | copy-start | bytes 294916
where the time goes:
time: 56.2 us; the launch traced here: 55.9 us
  Pallas kernels  50.4 us (90%)
  local copies, waits for them, and re-layouts  3.69 us (7%)
  other arithmetic  1.14 us (2%)
  between operations  0.66 us (1%)
    pallas_call x1, Pallas kernels, shards(): pl.pallas_call(functools.partial(kernel, nx, ny), out_shape=[jax.ShapeDty...  50.4 us
    unnamed x6, local copies, waits for them, and re-layouts  2.41 us
    unnamed x2, other arithmetic  1.14 us

commit v1 on v0

--- a/solution.py
+++ b/solution.py
@@ -39,31 +39,8 @@
     return 16 + k if k < 4 else 20 + j
 
 
-def split_table(table):
-    high = table.astype(ml_dtypes.bfloat16)
-    low = (table - high.astype(np.float64)).astype(ml_dtypes.bfloat16)
-    return high, low
-
-
 @functools.cache
 def tables():
-    derivative, weights = gll_tables()
-    grads = np.zeros((384, 208))
-    cube = np.zeros(384)
-    for i in range(5):
-        for j in range(5):
-            for k in range(5):
-                row = i * 25 + j * 5 + k
-                for d in range(3):
-                    cube[d * 128 + row] = weights[i] * weights[j] * weights[k]
-                for n in range(5):
-                    grads[row, place(k, j) * 8 + n] += derivative[i, n]
-                    grads[128 + row, place(k, n) * 8 + i] += derivative[j, n]
-                    grads[256 + row, place(n, j) * 8 + i] += derivative[k, n]
-    high, low = split_table(grads)
-    first = np.concatenate([high, high, low], axis=1)
-    high, low = split_table((grads[:, :200] * cube[:, None]).T)
-    second = np.concatenate([high, high, low], axis=1)
     spread = np.zeros((512, 512), ml_dtypes.bfloat16)
     pack = np.zeros((128, 128), ml_dtypes.bfloat16)
     for k in range(4):
@@ -71,7 +48,20 @@
             pack[4 * c + k, k * 32 + c] = 1
             for b in range(4):
                 spread[b * 128 + 4 * c + k, k * 128 + b * 32 + c] = 1
-    return first, second, spread, np.ascontiguousarray(spread.T), pack
+    return spread, np.ascontiguousarray(spread.T), pack
+
+
+def apply(matrix, v):
+    even0, odd0 = v[0] + v[4], v[0] - v[4]
+    even1, odd1 = v[1] + v[3], v[1] - v[3]
+    out = [None] * 5
+    for a in range(2):
+        row = matrix[a]
+        first = float(row[0] - row[4]) / 2 * odd0 + float(row[1] - row[3]) / 2 * odd1
+        second = float(row[0] + row[4]) / 2 * even0 + float(row[1] + row[3]) / 2 * even1 + float(row[2]) * v[2]
+        out[a], out[4 - a] = first + second, first - second
+    out[2] = float(matrix[2][0]) * odd0 + float(matrix[2][1]) * odd1
+    return out
 
 
 def halves(value):
@@ -95,8 +85,6 @@
     la_hbm,
     mu_hbm,
     level_hbm,
-    first_hbm,
-    second_hbm,
     spread_hbm,
     gather_hbm,
     pack_hbm,
@@ -104,11 +92,12 @@
     vo_hbm,
     u_vm,
     vim_vm,
+    la_raw,
+    mu_raw,
     la_vm,
     mu_vm,
+    mu_twice,
     level_vm,
-    first_vm,
-    second_vm,
     spread_vm,
     gather_vm,
     pack_vm,
@@ -126,8 +115,9 @@
     u_line,
     v_line,
     im_line,
-    u_split,
-    s_split,
+    grad_z,
+    stress_x,
+    f_new,
     f_kept,
     f_sum,
     pack_up,
@@ -171,10 +161,8 @@
             (im_hbm, vim_vm.at[3:4]),
             (spread_hbm, spread_vm),
             (pack_hbm, pack_vm),
-            (first_hbm, first_vm),
-            (la_hbm, la_vm.at[0:125]),
-            (mu_hbm, mu_vm.at[0:125]),
-            (second_hbm, second_vm),
+            (la_hbm, la_raw),
+            (mu_hbm, mu_raw),
             (level_hbm, level_vm),
             (gather_hbm, gather_vm),
         ]
@@ -275,10 +263,19 @@
         fill_own(3 + c, vim_vm.at[c])
     loads[3].wait()
     loads[4].wait()
-    for n in range(5, 11):
+    for n in range(5, 9):
         loads[n].wait()
-    la_vm[125:128, :] = jnp.zeros((3, 128), F32)
-    mu_vm[125:128, :] = jnp.zeros((3, 128), F32)
+    derivative, weights = gll_tables()
+    la_vm[...] = jnp.zeros_like(la_vm)
+    mu_vm[...] = jnp.zeros_like(mu_vm)
+    for k in range(5):
+        for j in range(5):
+            for i in range(5):
+                weight = float(weights[i] * weights[j] * weights[k])
+                row = (k * 5 + j) * 8 + i
+                la_vm[row : row + 1, :] = weight * la_raw[i, j, k]
+                mu_vm[row : row + 1, :] = weight * mu_raw[i, j, k]
+    mu_twice[...] = 2.0 * mu_vm[...]
 
     wait_halo(0)
     wait_halo(1)
@@ -313,38 +310,62 @@
                 below = pltpu.roll(u_all[c, group(j if j < 4 else 16), :], 127, 1)
                 u_all[c, group(20 + j), :] = jnp.where(depth < 31, below, 0.0)
 
+    def columns(matrix):
+        out = []
+        for n in range(5):
+            values = jnp.zeros((8, 128), F32)
+            for i in range(5):
+                values = jnp.where(sublane == i, float(matrix[i][n]), values)
+            out.append(values)
+        return out
+
+    def along_x(vectors, ref, c, row):
+        total = vectors[0] * jnp.broadcast_to(ref[c, row : row + 1, :], (8, 128))
+        for n in range(1, 5):
+            total = total + vectors[n] * jnp.broadcast_to(ref[c, row + n : row + n + 1, :], (8, 128))
+        return total
+
     def forces(s):
-        for c in range(3):
-            high, low = halves(u_all[c])
-            lanes = slice(c * 128, (c + 1) * 128)
-            u_split[0:208, lanes] = high
-            u_split[208:416, lanes] = low
-            u_split[416:624, lanes] = high
-        grads = jnp.dot(first_vm[...], u_split[...], preferred_element_type=F32)
-
-        def grad(c, d):
-            return grads[d * 128 : (d + 1) * 128, c * 128 : (c + 1) * 128]
-
-        first, second = la_vm[...], mu_vm[...]
-        pressure = first * (grad(0, 0) + grad(1, 1) + grad(2, 2))
-        for c in range(3):
-            for d in range(c, 3):
-                if c == d:
-                    stress = pressure + 2.0 * second * grad(c, c)
-                else:
-                    stress = second * (grad(c, d) + grad(d, c))
-                high, low = halves(stress)
-                for e, f in ((c, d), (d, c))[: 1 + (c != d)]:
-                    lanes = slice(e * 128, (e + 1) * 128)
-                    s_split[f * 128 : (f + 1) * 128, lanes] = high
-                    s_split[384 + f * 128 : 384 + (f + 1) * 128, lanes] = low
-                    s_split[768 + f * 128 : 768 + (f + 1) * 128, lanes] = high
-        out = jnp.dot(second_vm[...], s_split[...], preferred_element_type=F32)
+        forward, backward = columns(derivative), columns(derivative.T)
+        for c in range(3):
+            for j in range(5):
+                out = apply(derivative, [u_all[c, group(place(k, j)), :] for k in range(5)])
+                for k in range(5):
+                    grad_z[c, group(k * 5 + j), :] = out[k]
+        for k in range(5):
+            gy = [apply(derivative, [u_all[c, group(place(k, j)), :] for j in range(5)]) for c in range(3)]
+            stress_y = [[], [], []]
+            for j in range(5):
+                rows = group(k * 5 + j)
+                gx = [along_x(forward, u_all, c, place(k, j) * 8) for c in range(3)]
+                gz = [grad_z[c, rows, :] for c in range(3)]
+                first, second, twice = la_vm[rows, :], mu_vm[rows, :], mu_twice[rows, :]
+                pressure = first * (gx[0] + gy[1][j] + gz[2])
+                xy = second * (gy[0][j] + gx[1])
+                xz = second * (gz[0] + gx[2])
+                yz = second * (gz[1] + gy[2][j])
+                stress_x[0, rows, :] = pressure + twice * gx[0]
+                stress_x[1, rows, :] = xy
+                stress_x[2, rows, :] = xz
+                stress_y[0].append(xy)
+                stress_y[1].append(pressure + twice * gy[1][j])
+                stress_y[2].append(yz)
+                grad_z[0, rows, :] = xz
+                grad_z[1, rows, :] = yz
+                grad_z[2, rows, :] = pressure + twice * gz[2]
+            for c in range(3):
+                out = apply(derivative.T, stress_y[c])
+                for j in range(5):
+                    f_new[c, group(k * 5 + j), :] = out[j] + along_x(backward, stress_x, c, (k * 5 + j) * 8)
         least = jnp.where(s == 0, 0, jnp.where(s == 2, 1, 2))
-        active = level_vm[...] >= least
-        for c in range(3):
-            new = out[:, c * 128 : (c + 1) * 128]
-            f_kept[c] = jnp.where(active, new, f_kept[c])
+        active = jnp.broadcast_to(level_vm[...], (8, 128)) >= least
+        for c in range(3):
+            for j in range(5):
+                out = apply(derivative.T, [grad_z[c, group(k * 5 + j), :] for k in range(5)])
+                for k in range(5):
+                    new = f_new[c, group(k * 5 + j), :] + out[k]
+                    rows = group(place(k, j))
+                    f_kept[c, rows, :] = jnp.where(active, new, f_kept[c, rows, :])
 
     def assemble(s, last):
         for c in range(3):
@@ -523,21 +544,22 @@
 
 
 def shards(nx, ny, displacement, velocity, inverse_mass, lame_first, lame_second, level_map):
-    first, second, spread, gather, pack = (jnp.asarray(table) for table in tables())
+    spread, gather, pack = (jnp.asarray(table) for table in tables())
     vmem = pltpu.VMEM
     uo, vo = pl.pallas_call(
         functools.partial(kernel, nx, ny),
         out_shape=[jax.ShapeDtypeStruct((3, 64, 128), F32)] * 2,
-        in_specs=[pl.BlockSpec(memory_space=pl.ANY)] * 11,
+        in_specs=[pl.BlockSpec(memory_space=pl.ANY)] * 9,
         out_specs=[pl.BlockSpec(memory_space=pl.ANY)] * 2,
         scratch_shapes=[
             vmem((3, 64, 128), F32),
             vmem((4, 64, 128), F32),
-            vmem((128, 128), F32),
-            vmem((128, 128), F32),
+            vmem((5, 5, 5, 1, 128), F32),
+            vmem((5, 5, 5, 1, 128), F32),
+            vmem((200, 128), F32),
+            vmem((200, 128), F32),
+            vmem((200, 128), F32),
             vmem((1, 128), jnp.int32),
-            vmem((384, 624), BF16),
-            vmem((200, 1152), BF16),
             vmem((512, 512), BF16),
             vmem((512, 512), BF16),
             vmem((128, 128), BF16),
@@ -549,14 +571,15 @@
             vmem((8, 128), F32),
             vmem((4, 224, 128), F32),
             vmem((56, 128), F32),
-            vmem((3, 208, 128), F32),
+            vmem((3, 200, 128), F32),
             vmem((3, 128, 128), F32),
             vmem((128, 128), F32),
             vmem((24, 128), F32),
             vmem((24, 128), F32),
             vmem((8, 128), F32),
-            vmem((624, 384), BF16),
-            vmem((1152, 384), BF16),
+            vmem((3, 200, 128), F32),
+            vmem((3, 200, 128), F32),
+            vmem((3, 200, 128), F32),
             vmem((3, 200, 128), F32),
             vmem((3, 128, 128), F32),
             vmem((24, 128), F32),
@@ -569,7 +592,7 @@
             vmem((SUBSTEPS, 2, 24, 128), F32),
             vmem((3, 64, 128), F32),
             vmem((3, 64, 128), F32),
-            pltpu.SemaphoreType.DMA((11,)),
+            pltpu.SemaphoreType.DMA((9,)),
             pltpu.SemaphoreType.DMA((5,)),
             pltpu.SemaphoreType.DMA((5,)),
             pltpu.SemaphoreType.DMA((SUBSTEPS, 8)),
@@ -581,11 +604,9 @@
         displacement.reshape(3, 64, 128),
         velocity.reshape(3, 64, 128),
         inverse_mass.reshape(1, 64, 128),
-        lame_first.reshape(125, 128),
-        lame_second.reshape(125, 128),
+        lame_first,
+        lame_second,
         level_map,
-        first,
-        second,
         spread,
         gather,
         pack,

time: 56.2 us -> 51.1 us (0.909)
  Pallas kernels: 50.4 us -> 48.1 us
  local copies, waits for them, and re-layouts: 3.69 us -> 2.22 us
  other arithmetic: 1.14 us -> 0 us
    pallas_call x1, Pallas kernels: 50.4 us -> 48.1 us  [shards(): pl.pallas_call(functools.partial(kernel, nx, ny), out_shape=[jax.ShapeDty...]
    reshape x2 -> x0, local copies, waits for them, and re-layouts: 1.28 us -> none  [the longest x1 0.64 us: shards(): lame_first.reshape(125, 128)]
    unnamed x2 -> x0, other arithmetic: 1.14 us -> none
    unnamed x6 -> x4, local copies, waits for them, and re-layouts: 2.41 us -> 2.22 us
where the time goes in v1:
time: 51.1 us; the launch traced here: 50.9 us
  Pallas kernels  48.1 us (94%)
  local copies, waits for them, and re-layouts  2.22 us (4%)
  between operations  0.65 us (1%)
    pallas_call x1, Pallas kernels, shards(): pl.pallas_call(functools.partial(kernel, nx, ny), out_shape=[jax.ShapeDty...  48.1 us
    unnamed x4, local copies, waits for them, and re-layouts  2.22 us

profile of v1, /device:TPU:513, one launch (start us, length us, event | category | flops | bytes accessed | tf_op | source)
XLA Modules:
  0.0 50.9 jit_solution(15067130310586922116)
XLA Ops:
  0.6 48.1 %substeps.1 = (f32[3,64,128]{2,1,0:T(8,128)}, f32[3,64,128]{2,1,0:T(8,128)}) custom-call(f32[3,64,128]{2,1,0:T(8,128)} %bitcast.5, f32[3,64,128]{2,1,0:T(8,128)} %bitcast.6, f32[1,64,128]{2,1,0:T(8,128)} %bitcast.9, f32[5,5,5,1,128]{4,3,2,1,0:T(1,128)} %la_hbm.1, f32[5,5,5,1,128]{4,3,2,1,0:T(1,128)} %mu_hbm.1, s32[1,128]{1,0:T(1,128)} %level_hbm.1, ...), custom_call_target="tpu_custom_call" | custom-call | tf_op jit(solution)/shard_map/substeps/pallas_call | solution.py:549
  48.7 0.0 copy-start
  48.7 1.6 %copy.13 = f32[3,4,16,128]{3,2,1,0:T(8,128)} copy(f32[3,4,16,128]{3,2,1,0:T(8,128)} %bitcast.8) | data formatting | bytes 196608
  50.3 0.0 copy-done
  50.3 0.6 %copy.14 = f32[3,4,16,128]{3,2,1,0:T(8,128)} copy(f32[3,4,16,128]{3,2,1,0:T(8,128)S(1)} %bitcast.7) | data formatting | bytes 196608
Async XLA Ops:
  48.7 1.6 %copy-start = (f32[3,64,128]{2,1,0:T(8,128)S(1)}, f32[3,64,128]{2,1,0:T(8,128)}, u32[]{:S(2)}) copy-start(f32[3,64,128]{2,1,0:T(8,128)} %get-tuple-element.5) | copy-start | bytes 294916

commit v2 on v1

--- a/solution.py
+++ b/solution.py
@@ -88,8 +88,8 @@
     spread_hbm,
     gather_hbm,
     pack_hbm,
-    uo_hbm,
-    vo_hbm,
+    uo_vm,
+    vo_vm,
     u_vm,
     vim_vm,
     la_raw,
@@ -128,8 +128,6 @@
     recv_x,
     recv_d,
     recv_y,
-    uo_vm,
-    vo_vm,
     load_sem,
     halo_send_sem,
     halo_recv_sem,
@@ -521,12 +519,6 @@
                 row = ((a * 3 + c) * 4 + j) * 8
                 for b in range(4):
                     target[c, pl.ds(4 * b + j, 4, stride=16), :] = result[row : row + 4, b * 128 : (b + 1) * 128]
-    stores = [
-        pltpu.make_async_copy(uo_vm, uo_hbm, load_sem.at[0]),
-        pltpu.make_async_copy(vo_vm, vo_hbm, load_sem.at[1]),
-    ]
-    for copy in stores:
-        copy.start()
     for copy, to in zip(halos, halo_to):
 
         @pl.when(present(*to))
@@ -539,7 +531,16 @@
 
     lax.fori_loop(0, SUBSTEPS - 1, drain, 0)
     finish(exchange(SUBSTEPS - 1, True))
-    for copy in stores:
+
+
+def write_out(u_ref, v_ref, uo_ref, vo_ref, sem):
+    copies = [
+        pltpu.make_async_copy(u_ref, uo_ref, sem.at[0]),
+        pltpu.make_async_copy(v_ref, vo_ref, sem.at[1]),
+    ]
+    for copy in copies:
+        copy.start()
+    for copy in copies:
         copy.wait()
 
 
@@ -549,8 +550,8 @@
     uo, vo = pl.pallas_call(
         functools.partial(kernel, nx, ny),
         out_shape=[jax.ShapeDtypeStruct((3, 64, 128), F32)] * 2,
-        in_specs=[pl.BlockSpec(memory_space=pl.ANY)] * 9,
-        out_specs=[pl.BlockSpec(memory_space=pl.ANY)] * 2,
+        in_specs=[pl.BlockSpec(memory_space=pltpu.HBM)] * 9,
+        out_specs=[pl.BlockSpec(memory_space=pltpu.VMEM)] * 2,
         scratch_shapes=[
             vmem((3, 64, 128), F32),
             vmem((4, 64, 128), F32),
@@ -590,27 +591,39 @@
             vmem((SUBSTEPS, 2, 56, 128), F32),
             vmem((SUBSTEPS, 4, 8, 128), F32),
             vmem((SUBSTEPS, 2, 24, 128), F32),
-            vmem((3, 64, 128), F32),
-            vmem((3, 64, 128), F32),
             pltpu.SemaphoreType.DMA((9,)),
             pltpu.SemaphoreType.DMA((5,)),
             pltpu.SemaphoreType.DMA((5,)),
             pltpu.SemaphoreType.DMA((SUBSTEPS, 8)),
             pltpu.SemaphoreType.DMA((SUBSTEPS, 8)),
         ],
-        compiler_params=pltpu.CompilerParams(collective_id=0, has_side_effects=True),
+        compiler_params=pltpu.CompilerParams(collective_id=0, has_side_effects=True, vmem_limit_bytes=16 * 2**20),
         name="substeps",
     )(
-        displacement.reshape(3, 64, 128),
-        velocity.reshape(3, 64, 128),
-        inverse_mass.reshape(1, 64, 128),
-        lame_first,
-        lame_second,
-        level_map,
-        spread,
-        gather,
-        pack,
+        *(
+            pltpu.with_memory_space_constraint(array, pltpu.HBM)
+            for array in (
+                displacement.reshape(3, 64, 128),
+                velocity.reshape(3, 64, 128),
+                inverse_mass.reshape(1, 64, 128),
+                lame_first,
+                lame_second,
+                level_map,
+                spread,
+                gather,
+                pack,
+            )
+        )
     )
+    uo, vo = pl.pallas_call(
+        write_out,
+        out_shape=[jax.ShapeDtypeStruct((3, 64, 128), F32)] * 2,
+        in_specs=[pl.BlockSpec(memory_space=pl.ANY)] * 2,
+        out_specs=[pl.BlockSpec(memory_space=pl.ANY)] * 2,
+        scratch_shapes=[pltpu.SemaphoreType.DMA((2,))],
+        compiler_params=pltpu.CompilerParams(vmem_limit_bytes=2**20),
+        name="write_out",
+    )(uo, vo)
     return uo.reshape(3, 4, 16, 128), vo.reshape(3, 4, 16, 128)
 
 

time: 51.1 us -> 49 us (0.959)
  local copies, waits for them, and re-layouts: 2.22 us -> 0 us
    unnamed x4 -> x0, local copies, waits for them, and re-layouts: 2.22 us -> none
    pallas_call x0 -> x1, Pallas kernels: none -> 0.69 us  [shards(): pl.pallas_call(write_out, out_shape=[jax.ShapeDtypeStruct((3, 64, 128), F...]
    pallas_call x1, Pallas kernels: 48.1 us -> 47.5 us  [shards(): pl.pallas_call(functools.partial(kernel, nx, ny), out_shape=[jax.ShapeDty...]
where the time goes in v2:
time: 49 us; the launch traced here: 48.8 us
  Pallas kernels  48.2 us (98%)
  between operations  0.64 us (1%)
    pallas_call x1, Pallas kernels, shards(): pl.pallas_call(functools.partial(kernel, nx, ny), out_shape=[jax.ShapeDty...  47.5 us

profile of v2, /device:TPU:513, one launch (start us, length us, event | category | flops | bytes accessed | tf_op | source)
XLA Modules:
  0.0 48.8 jit_solution(11756853947404665552)
XLA Ops:
  0.6 47.5 %substeps.1 = (f32[3,64,128]{2,1,0:T(8,128)S(1)}, f32[3,64,128]{2,1,0:T(8,128)S(1)}) custom-call(f32[3,64,128]{2,1,0:T(8,128)} %bitcast.5, f32[3,64,128]{2,1,0:T(8,128)} %bitcast.6, f32[1,64,128]{2,1,0:T(8,128)} %bitcast.7, f32[5,5,5,1,128]{4,3,2,1,0:T(1,128)} %la_hbm.1, f32[5,5,5,1,128]{4,3,2,1,0:T(1,128)} %mu_hbm.1, s32[1,128]{1,0:T(1,128)} %level_hbm.1, ...), custom_call_target="tpu_custom_call" | custom-call | tf_op jit(solution)/shard_map/substeps/pallas_call | solution.py:550
  48.1 0.7 %write_out.1 = (f32[3,64,128]{2,1,0:T(8,128)}, f32[3,64,128]{2,1,0:T(8,128)}) custom-call(f32[3,64,128]{2,1,0:T(8,128)S(1)} %get-tuple-element.6.u_ref, f32[3,64,128]{2,1,0:T(8,128)S(1)} %get-tuple-element.7.v_ref), custom_call_target="tpu_custom_call" | custom-call | tf_op jit(solution)/shard_map/write_out/pallas_call | solution.py:618

commit v3 on v2

--- a/solution.py
+++ b/solution.py
@@ -108,6 +108,7 @@
     halo_c_send,
     halo_c,
     x_own,
+    x_face,
     x_line,
     u_all,
     v_own,
@@ -170,6 +171,7 @@
 
     x_own[...] = jnp.zeros_like(x_own)
     x_line[...] = jnp.zeros_like(x_line)
+    x_face[...] = jnp.zeros_like(x_face)
     u_all[...] = jnp.zeros_like(u_all)
 
     for n, (dx, dy) in enumerate(NEIGHBOURS):
@@ -247,13 +249,14 @@
                 row = (c * 4 + j) * 8
                 x_own[b, row : row + 4, :] = source[pl.ds(4 * b + j, 4, stride=16), :]
 
-    def fill_far(c, source):
-        for b in range(4):
-            x_own[b, pl.ds(c * 32 + 4, 4, stride=8), :] = source[4 * b : 4 * b + 4, :]
-
-    def spread(first_row, rows):
-        wide = jnp.concatenate([x_own[b, first_row : first_row + rows, :] for b in range(4)], axis=1)
-        return permute(wide, spread_vm[...])
+    def wide(ref, first_row, rows):
+        return jnp.concatenate([ref[b, first_row : first_row + rows, :] for b in range(4)], axis=1)
+
+    def far_rows(source, count):
+        for c in range(count):
+            for b in range(4):
+                x_face[b, c * 4 : c * 4 + 4, :] = source[c, 4 * b : 4 * b + 4, :]
+        return permute(wide(x_face, 0, 16), spread_vm[...])
 
     for c in range(3):
         fill_own(c, u_vm.at[c])
@@ -275,24 +278,32 @@
                 mu_vm[row : row + 1, :] = weight * mu_raw[i, j, k]
     mu_twice[...] = 2.0 * mu_vm[...]
 
-    wait_halo(0)
-    wait_halo(1)
-    wait_halo(2)
-    for c in range(3):
-        fill_far(c, halo_u.at[c])
+    nodes = permute(wide(x_own, 0, 224), spread_vm[...])
     for c in range(7):
-        x_line[c * 8 : c * 8 + 4, :] = halo_y[4 * c : 4 * c + 4, :]
-        x_line[c * 8 + 4 : c * 8 + 5, :] = halo_c[c : c + 1, :]
-    nodes = spread(0, 96)
-    for c in range(3):
         for j in range(4):
             for k in range(4):
                 row = (c * 4 + j) * 8
-                u_all[c, (k * 4 + j) * 8 : (k * 4 + j + 1) * 8, :] = nodes[row : row + 8, k * 128 : (k + 1) * 128]
-    lines = permute(x_line[...], pack_vm[...])
-    u_line[...] = lines[0:24]
-    v_line[...] = lines[24:48]
-    im_line[...] = TIME_STEP * lines[48:56]
+                rows = pl.ds((k * 4 + j) * 8, 8)
+                value = nodes[row : row + 8, k * 128 : (k + 1) * 128]
+                if c < 3:
+                    u_all[c, rows, :] = value
+                elif c < 6:
+                    v_own[c - 3, rows, :] = value
+                else:
+                    im_own[rows, :] = TIME_STEP * value
+
+    wait_halo(2)
+    for c in range(7):
+        x_line[c * 8 : c * 8 + 4, :] = halo_y[4 * c : 4 * c + 4, :]
+    wait_halo(0)
+    wait_halo(1)
+    face = far_rows(halo_u, 3)
+    for c in range(3):
+        for k in range(4):
+            u_all[c, pl.ds(k * 32 + 4, 4, stride=8), :] = face[c * 4 : c * 4 + 4, k * 128 : (k + 1) * 128]
+    for c in range(7):
+        x_line[c * 8 + 4 : c * 8 + 5, :] = halo_c[c : c + 1, :]
+    u_line[...] = permute(x_line[0:24, :], pack_vm[...])
 
     def group(p):
         return pl.ds(p * 8, 8)
@@ -433,52 +444,61 @@
             def _():
                 copy.wait_send()
 
-    def advance(s, last):
-        for c in range(3):
-            near = recv_y[s, 0, c * 8 : c * 8 + 8, :]
-            near = near + jnp.where(sublane == 0, recv_d[s, DPP - 2, c : c + 1, :], 0.0)
-            if not last:
-                near = near + jnp.where(sublane == 4, recv_d[s, DMP - 2, c : c + 1, :], 0.0)
+    def before_x(s, last):
+        for c in range(3):
+            rows = slice(c * 8, c * 8 + 8)
+            near = recv_y[s, 0, rows, :]
             for k in range(4):
                 part = pltpu.roll(near, 128 - 32 * k, 1) if k else near
                 f_sum[c, group(4 * k), :] = f_sum[c, group(4 * k), :] + jnp.where(column == 0, part, 0.0)
-            f_sum[c, pl.ds(0, 16, stride=8), :] = f_sum[c, pl.ds(0, 16, stride=8), :] + recv_x[s, XF, c * 16 : c * 16 + 16, :]
-            if not last:
-                f_sum[c, pl.ds(4, 16, stride=8), :] = (
-                    f_sum[c, pl.ds(4, 16, stride=8), :] + recv_x[s, XB, c * 16 : c * 16 + 16, :]
-                )
-        for c in range(3):
             v = v_own[c] - im_own[...] * f_sum[c]
             v_own[c] = v
             u_all[c, 0:128, :] = u_all[c, 0:128, :] + TIME_STEP * v
-        if last:
-            return
+            if not last:
+                v = v_line[rows, :] - im_line[...] * (pack_up[rows, :] + recv_y[s, 1, rows, :])
+                v_line[rows, :] = v
+                u_line[rows, :] = u_line[rows, :] + TIME_STEP * v
+
+    def with_corner(s, n, corner):
+        for k in range(4):
+            value = recv_d[s, corner - 2]
+            part = pltpu.roll(value, 128 - 32 * k, 1) if k else value
+            rows = pl.ds(4 * k, 3, stride=16)
+            recv_x[s, n, rows, :] = recv_x[s, n, rows, :] + jnp.where(column == 0, part, 0.0)[0:3]
+
+    def after_x(s):
+        for n, corner, i in ((XF, DPP, 0), (XB, DMP, 4)):
+            with_corner(s, n, corner)
+            rows = pl.ds(i, 16, stride=8)
+            scale = im_own[rows, :]
+            for c in range(3):
+                change = scale * recv_x[s, n, c * 16 : c * 16 + 16, :]
+                v_own[c, rows, :] = v_own[c, rows, :] - change
+                u_all[c, rows, :] = u_all[c, rows, :] - TIME_STEP * change
         for c in range(3):
             rows = slice(c * 8, c * 8 + 8)
-            far = pack_up[rows, :] + recv_y[s, 1, rows, :]
             left = recv_x[s, XF, 48 + c : 49 + c, :] + recv_d[s, DPM - 2, c : c + 1, :]
             right = recv_x[s, XB, 48 + c : 49 + c, :] + recv_d[s, DMM - 2, c : c + 1, :]
-            far = far + jnp.where(sublane == 0, left, 0.0) + jnp.where(sublane == 4, right, 0.0)
-            v = v_line[rows, :] - im_line[...] * far
-            v_line[rows, :] = v
-            u_line[rows, :] = u_line[rows, :] + TIME_STEP * v
+            far = jnp.where(sublane == 0, left, jnp.where(sublane == 4, right, 0.0))
+            change = im_line[...] * far
+            v_line[rows, :] = v_line[rows, :] - change
+            u_line[rows, :] = u_line[rows, :] - TIME_STEP * change
         expand()
 
     def late_nodes():
+        v_line[...] = permute(x_line[24:48, :], pack_vm[...])
+        im_line[...] = TIME_STEP * permute(x_line[48:56, :], pack_vm[...])
         wait_halo(3)
         wait_halo(4)
+        face = far_rows(halo_vim, 4)
         for c in range(4):
-            fill_far(3 + c, halo_vim.at[c])
-        values = spread(96, 128)
-        for c in range(4):
-            for j in range(4):
-                for k in range(4):
-                    row = (c * 4 + j) * 8
-                    value = values[row : row + 8, k * 128 : (k + 1) * 128]
-                    if c < 3:
-                        v_own[c, group(k * 4 + j), :] = value
-                    else:
-                        im_own[group(k * 4 + j), :] = TIME_STEP * value
+            for k in range(4):
+                rows = pl.ds(k * 32 + 4, 4, stride=8)
+                value = face[c * 4 : c * 4 + 4, k * 128 : (k + 1) * 128]
+                if c < 3:
+                    v_own[c, rows, :] = value
+                else:
+                    im_own[rows, :] = TIME_STEP * value
 
     expand()
     forces(0)
@@ -486,16 +506,20 @@
     copies = exchange(0, False)
     start(copies)
     late_nodes()
-    arrive(copies)
-    advance(0, False)
+    arrive(copies[6:])
+    before_x(0, False)
+    arrive(copies[:6])
+    after_x(0)
 
     def substep(s, carry):
         forces(s)
         assemble(s, False)
         copies = exchange(s, False)
         start(copies)
-        arrive(copies)
-        advance(s, False)
+        arrive(copies[6:])
+        before_x(s, False)
+        arrive(copies[:6])
+        after_x(s)
         return carry
 
     lax.fori_loop(1, SUBSTEPS - 1, substep, 0)
@@ -504,8 +528,8 @@
     assemble(s, True)
     copies = exchange(s, True)
     start(copies)
-    arrive(copies)
-    advance(s, True)
+    arrive(copies[2:])
+    before_x(s, True)
 
     rows = []
     for source in (u_all, v_own):
@@ -519,6 +543,21 @@
                 row = ((a * 3 + c) * 4 + j) * 8
                 for b in range(4):
                     target[c, pl.ds(4 * b + j, 4, stride=16), :] = result[row : row + 4, b * 128 : (b + 1) * 128]
+
+    arrive(copies[:2])
+    with_corner(s, XF, DPP)
+    scale = im_own[pl.ds(0, 16, stride=8), :]
+    for c in range(3):
+        change = scale * recv_x[s, XF, c * 16 : c * 16 + 16, :]
+        for k in range(4):
+            x_face[k, c * 4 : c * 4 + 4, :] = change[4 * k : 4 * k + 4]
+    result = permute(wide(x_face, 0, 16), gather_vm[...])
+    for c in range(3):
+        for b in range(4):
+            rows = slice(4 * b, 4 * b + 4)
+            value = result[c * 4 : c * 4 + 4, b * 128 : (b + 1) * 128]
+            vo_vm[c, rows, :] = vo_vm[c, rows, :] - value
+            uo_vm[c, rows, :] = uo_vm[c, rows, :] - TIME_STEP * value
     for copy, to in zip(halos, halo_to):
 
         @pl.when(present(*to))
@@ -571,6 +610,7 @@
             vmem((8, 128), F32),
             vmem((8, 128), F32),
             vmem((4, 224, 128), F32),
+            vmem((4, 16, 128), F32),
             vmem((56, 128), F32),
             vmem((3, 200, 128), F32),
             vmem((3, 128, 128), F32),

time: 49 us -> 48.7 us (level)
  no operation moved by 1% of the time
where the time goes in v3:
time: 48.7 us; the launch traced here: 48.5 us
  Pallas kernels  47.9 us (98%)
  between operations  0.64 us (1%)
    pallas_call x1, Pallas kernels, shards(): pl.pallas_call(functools.partial(kernel, nx, ny), out_shape=[jax.ShapeDty...  47.2 us

profile of v3, /device:TPU:513, one launch (start us, length us, event | category | flops | bytes accessed | tf_op | source)
XLA Modules:
  0.0 48.5 jit_solution(50564308905742434)
XLA Ops:
  0.6 47.2 %substeps.1 = (f32[3,64,128]{2,1,0:T(8,128)S(1)}, f32[3,64,128]{2,1,0:T(8,128)S(1)}) custom-call(f32[3,64,128]{2,1,0:T(8,128)} %bitcast.5, f32[3,64,128]{2,1,0:T(8,128)} %bitcast.6, f32[1,64,128]{2,1,0:T(8,128)} %bitcast.7, f32[5,5,5,1,128]{4,3,2,1,0:T(1,128)} %la_hbm.1, f32[5,5,5,1,128]{4,3,2,1,0:T(1,128)} %mu_hbm.1, s32[1,128]{1,0:T(1,128)} %level_hbm.1, ...), custom_call_target="tpu_custom_call" | custom-call | tf_op jit(solution)/shard_map/substeps/pallas_call | solution.py:589
  47.8 0.7 %write_out.1 = (f32[3,64,128]{2,1,0:T(8,128)}, f32[3,64,128]{2,1,0:T(8,128)}) custom-call(f32[3,64,128]{2,1,0:T(8,128)S(1)} %get-tuple-element.6.u_ref, f32[3,64,128]{2,1,0:T(8,128)S(1)} %get-tuple-element.7.v_ref), custom_call_target="tpu_custom_call" | custom-call | tf_op jit(solution)/shard_map/write_out/pallas_call | solution.py:658

commit v4 on v3

--- a/solution.py
+++ b/solution.py
@@ -544,6 +544,18 @@
                 for b in range(4):
                     target[c, pl.ds(4 * b + j, 4, stride=16), :] = result[row : row + 4, b * 128 : (b + 1) * 128]
 
+    for copy, to in zip(halos, halo_to):
+
+        @pl.when(present(*to))
+        def _():
+            copy.wait_send()
+
+    def drain(s, carry):
+        finish(exchange(s, False))
+        return carry
+
+    lax.fori_loop(0, SUBSTEPS - 1, drain, 0)
+
     arrive(copies[:2])
     with_corner(s, XF, DPP)
     scale = im_own[pl.ds(0, 16, stride=8), :]
@@ -558,17 +570,6 @@
             value = result[c * 4 : c * 4 + 4, b * 128 : (b + 1) * 128]
             vo_vm[c, rows, :] = vo_vm[c, rows, :] - value
             uo_vm[c, rows, :] = uo_vm[c, rows, :] - TIME_STEP * value
-    for copy, to in zip(halos, halo_to):
-
-        @pl.when(present(*to))
-        def _():
-            copy.wait_send()
-
-    def drain(s, carry):
-        finish(exchange(s, False))
-        return carry
-
-    lax.fori_loop(0, SUBSTEPS - 1, drain, 0)
     finish(exchange(SUBSTEPS - 1, True))
 
 

time: 48.7 us -> 48.6 us (level)
  no operation moved by 1% of the time
where the time goes in v4:
time: 48.6 us; the launch traced here: 48.5 us
  Pallas kernels  47.8 us (98%)
  between operations  0.64 us (1%)
    pallas_call x1, Pallas kernels, shards(): pl.pallas_call(functools.partial(kernel, nx, ny), out_shape=[jax.ShapeDty...  47.1 us

profile of v4, /device:TPU:513, one launch (start us, length us, event | category | flops | bytes accessed | tf_op | source)
XLA Modules:
  0.0 48.5 jit_solution(9568970081079876484)
XLA Ops:
  0.6 47.1 %substeps.1 = (f32[3,64,128]{2,1,0:T(8,128)S(1)}, f32[3,64,128]{2,1,0:T(8,128)S(1)}) custom-call(f32[3,64,128]{2,1,0:T(8,128)} %bitcast.5, f32[3,64,128]{2,1,0:T(8,128)} %bitcast.6, f32[1,64,128]{2,1,0:T(8,128)} %bitcast.7, f32[5,5,5,1,128]{4,3,2,1,0:T(1,128)} %la_hbm.1, f32[5,5,5,1,128]{4,3,2,1,0:T(1,128)} %mu_hbm.1, s32[1,128]{1,0:T(1,128)} %level_hbm.1, ...), custom_call_target="tpu_custom_call" | custom-call | tf_op jit(solution)/shard_map/substeps/pallas_call | solution.py:590
  47.8 0.7 %write_out.1 = (f32[3,64,128]{2,1,0:T(8,128)}, f32[3,64,128]{2,1,0:T(8,128)}) custom-call(f32[3,64,128]{2,1,0:T(8,128)S(1)} %get-tuple-element.6.u_ref, f32[3,64,128]{2,1,0:T(8,128)S(1)} %get-tuple-element.7.v_ref), custom_call_target="tpu_custom_call" | custom-call | tf_op jit(solution)/shard_map/write_out/pallas_call | solution.py:659
